TPU v7x, 32 devices: a whole 2x2x4 slice. The times are simulated.
32 devices in a mesh: ctx: 8 (over z, core), fsdp: 4 (over y, x).
Axes of the slice: x: 2, y: 2, z: 4, core: 2. Of those that a mesh axis runs over, the one named last changes fastest.
Arguments:
- inputs: bfloat16 [4096, 5376], P('ctx'), may hold values from -400 to 400
- output_cotangent: bfloat16 [4096, 4096], P('ctx', 'fsdp'), may hold values from -96 to 96
- w_query: bfloat16 [5376, 4096], P('ctx', 'fsdp'), may hold values from -0.078125 to 0.078125
- key_projection: bfloat16 [5376, 2048], P('ctx', 'fsdp'), may hold values from -0.078125 to 0.078125
- value_projection: bfloat16 [5376, 2048], P('ctx', 'fsdp'), may hold values from -0.078125 to 0.078125
- norm_gain: float32 [5376], replicated, may hold values from 0.25 to 1.75
- q_gain: float32 [128], replicated, may hold values from 0.25 to 1.75
- key_norm_gain: float32 [128], replicated, may hold values from 0.25 to 1.75
- half_lengths: int32 [4], replicated, may hold values from 1 to 3072, 4096 in all
Outputs:
- grad_inputs: bfloat16 [4096, 5376], P('ctx', 'fsdp')
- grad_w_query: bfloat16 [5376, 4096], P('ctx', 'fsdp')
- grad_w_key: bfloat16 [5376, 2048], P('ctx', 'fsdp')
- grad_w_value: bfloat16 [5376, 2048], P('ctx', 'fsdp')
- grad_norm_gain: float32 [5376], P(('fsdp', 'ctx'))
- grad_q_gain: float32 [128], replicated
- grad_k_gain: float32 [128], replicated
- norm_row_dots: float32 [4096], P('ctx')
Inputs may be any that keep to these rules, and one draw needn't show every extreme that they name: `half_lengths`: the halves add up to 4096 tokens, and the longest holds exactly 3072.
All inputs are finite; a program needn't handle non-finite values.
Results may differ from a plain program's by a relative error of at most 0.035.
Values may be sent and summed in bfloat16 or wider, within the bound.
No kernel may reach another device: no remote copies, remote signals or barrier semaphores. Data moves between devices by JAX's collectives and lax.ppermute only.
A program may use at most 192 MiB of HBM per device.

v0:
```python
import jax
import jax.numpy as jnp
from jax import lax
from jax.sharding import PartitionSpec as P

WIN = 1024
REACH = 2


epsilon = 1e-06
query_scale = 168.0 ** (-0.5)


def from_behind(value, axis, steps):
    count = lax.axis_size(axis)
    initial, last = (max(0, -steps), min(count, count - steps))
    return lax.ppermute(value, axis, [(source, source + steps) for source in range(initial, last)])


def head_normalize(projected, head_count, head_dim):
    shaped = projected.reshape(projected.shape[0], head_count, head_dim)
    inverse = lax.rsqrt(jnp.mean(shaped * shaped, axis=2, keepdims=True) + epsilon)
    return (shaped * inverse, inverse)


def head_normalize_backward(upstream_grad, normal_part, inverse, gain_vector):
    upstream = upstream_grad * gain_vector
    return inverse * (
        upstream - normal_part * jnp.mean(upstream * normal_part, axis=2, keepdims=True)
    )


def on_device(
    inputs,
    output_cotangent,
    w_query,
    key_projection,
    value_projection,
    norm_gain,
    q_gain,
    key_norm_gain,
    half_lengths,
):
    tokens = inputs.shape[0]
    model_width = inputs.shape[1]
    head_dim = q_gain.shape[0]
    q_cols = w_query.shape[1]
    kv_cols = key_projection.shape[1]
    q_heads = q_cols // head_dim
    kv_heads = kv_cols // head_dim
    queries_per_group = q_heads // kv_heads
    ctx_count = lax.axis_size("ctx")
    ctx_index = lax.axis_index("ctx")
    first_row = ctx_index * tokens
    grad_scale = float(tokens * ctx_count) ** (-0.5)
    contract_cols = (((1,), (1,)), ((), ()))
    contract_rows = (((0,), (0,)), ((), ()))
    widened = inputs.astype(jnp.float32)
    inv_rms = lax.rsqrt(jnp.mean(widened * widened, axis=1, keepdims=True) + epsilon)
    x_hat = widened * inv_rms
    normed = (x_hat * norm_gain).astype(jnp.bfloat16)
    stacked = jnp.concatenate([w_query, key_projection, value_projection], axis=1)
    projected = jnp.dot(
        normed,
        lax.all_gather(stacked, "ctx", axis=0, tiled=True),
        preferred_element_type=jnp.float32,
    )
    q_raw = projected[:, :q_cols]
    key_unnormed = projected[:, q_cols : q_cols + kv_cols]
    value_rows = projected[:, q_cols + kv_cols :].astype(jnp.bfloat16)
    query_normalized, q_inverse = head_normalize(q_raw, q_heads, head_dim)
    key_normalized, key_inverse_rms = head_normalize(key_unnormed, kv_heads, head_dim)
    query_multiplier = q_gain * query_scale
    query_rows = (
        (query_normalized * query_multiplier)
        .astype(jnp.bfloat16)
        .reshape(tokens, kv_heads, queries_per_group, head_dim)
    )
    key_rows = (key_normalized * key_norm_gain).astype(jnp.bfloat16)
    per_head_grads = output_cotangent.reshape(tokens, kv_heads, queries_per_group, head_dim)
    packed_kv = jnp.concatenate([key_rows.reshape(tokens, kv_cols), value_rows], axis=1)
    remote = [from_behind(packed_kv, "ctx", offset) for offset in range(1, REACH + 1)]
    key_tiles = [packed_kv] + remote
    segment_ends = jnp.cumsum(half_lengths)
    local_rows = lax.iota(jnp.int32, tokens)

    def segment_of(start_row):
        positions = start_row + local_rows
        return jnp.sum((segment_ends[None, :] <= positions[:, None]).astype(jnp.int32), axis=1)

    query_pos = first_row + local_rows
    query_seg = segment_of(first_row)

    def split_tile(key_tile):
        tile_keys = key_tile[:, :kv_cols].reshape(tokens, kv_heads, head_dim)
        tile_values = key_tile[:, kv_cols:].reshape(tokens, kv_heads, head_dim)
        return (tile_keys, tile_values)

    def first_pass(key_tile, allowed):
        tile_keys, tile_values = split_tile(key_tile)
        scores = jnp.einsum(
            "ikgd,jkd->kgij", query_rows, tile_keys, preferred_element_type=jnp.float32
        )
        weights = jnp.where(allowed, jnp.exp(scores), 0.0)
        numer = jnp.einsum(
            "kgij,jkd->ikgd",
            weights.astype(jnp.bfloat16),
            tile_values,
            preferred_element_type=jnp.float32,
        )
        return (jnp.sum(weights, axis=3), numer, weights)

    def skip_first(key_tile, allowed):
        return (
            jnp.zeros((kv_heads, queries_per_group, tokens), jnp.float32),
            jnp.zeros((tokens, kv_heads, queries_per_group, head_dim), jnp.float32),
            jnp.zeros((kv_heads, queries_per_group, tokens, tokens), jnp.float32),
        )

    totals = jnp.zeros((kv_heads, queries_per_group, tokens), jnp.float32)
    numer_sum = jnp.zeros((tokens, kv_heads, queries_per_group, head_dim), jnp.float32)
    tile_weights = []
    tile_active = []
    for offset, key_tile in enumerate(key_tiles):
        key_start = first_row - offset * tokens
        key_pos = key_start + local_rows
        key_seg = segment_of(key_start)
        distance = query_pos[:, None] - key_pos[None, :]
        allowed = (
            (query_seg[:, None] == key_seg[None, :])
            & (distance >= 0)
            & (distance < WIN)
            & (key_pos[None, :] >= 0)
        )
        active = (key_start + tokens > 0) & (key_seg[tokens - 1] >= query_seg[0])
        part_totals, part_numer, weights = lax.cond(
            active, first_pass, skip_first, key_tile, allowed
        )
        totals = totals + part_totals
        numer_sum = numer_sum + part_numer
        tile_weights.append(weights)
        tile_active.append(active)
    attn_out = numer_sum / jnp.transpose(totals, (2, 0, 1))[..., None]
    delta_rows = jnp.transpose(
        jnp.sum(per_head_grads.astype(jnp.float32) * attn_out, axis=3), (1, 2, 0)
    )

    def second_pass(key_tile, weights):
        tile_keys, tile_values = split_tile(key_tile)
        probs = weights / totals[..., None]
        d_probs = jnp.einsum(
            "ikgd,jkd->kgij", per_head_grads, tile_values, preferred_element_type=jnp.float32
        )
        d_scores = (probs * (d_probs - delta_rows[..., None])).astype(jnp.bfloat16)
        d_query = jnp.einsum(
            "kgij,jkd->ikgd", d_scores, tile_keys, preferred_element_type=jnp.float32
        )
        d_key = jnp.einsum(
            "kgij,ikgd->jkd", d_scores, query_rows, preferred_element_type=jnp.float32
        )
        d_value = jnp.einsum(
            "kgij,ikgd->jkd",
            probs.astype(jnp.bfloat16),
            per_head_grads,
            preferred_element_type=jnp.float32,
        )
        return (
            d_query,
            jnp.concatenate(
                [d_key.reshape(tokens, kv_cols), d_value.reshape(tokens, kv_cols)], axis=1
            ),
        )

    def skip_second(key_tile, weights):
        return (
            jnp.zeros((tokens, kv_heads, queries_per_group, head_dim), jnp.float32),
            jnp.zeros((tokens, 2 * kv_cols), jnp.float32),
        )

    d_query_sum = jnp.zeros((tokens, kv_heads, queries_per_group, head_dim), jnp.float32)
    kv_grad_parts = []
    for offset, key_tile in enumerate(key_tiles):
        d_query, kv_grad = lax.cond(
            tile_active[offset], second_pass, skip_second, key_tile, tile_weights[offset]
        )
        d_query_sum = d_query_sum + d_query
        kv_grad_parts.append(kv_grad)
    kv_grad_total = kv_grad_parts[0]
    for offset in range(1, REACH + 1):
        kv_grad_total = kv_grad_total + from_behind(
            kv_grad_parts[offset].astype(jnp.bfloat16), "ctx", -offset
        ).astype(jnp.float32)
    d_queries = d_query_sum.reshape(tokens, q_heads, head_dim)
    key_grads = kv_grad_total[:, :kv_cols].reshape(tokens, kv_heads, head_dim)
    dq16 = (
        head_normalize_backward(d_queries, query_normalized, q_inverse, query_multiplier)
        .reshape(tokens, q_cols)
        .astype(jnp.bfloat16)
    )
    key_grads_half16 = (
        head_normalize_backward(key_grads, key_normalized, key_inverse_rms, key_norm_gain)
        .reshape(tokens, kv_cols)
        .astype(jnp.bfloat16)
    )
    value_grads_half16 = kv_grad_total[:, kv_cols:].astype(jnp.bfloat16)
    d_stacked = jnp.concatenate([dq16, key_grads_half16, value_grads_half16], axis=1)
    head_part = lax.dot_general(
        d_stacked,
        lax.all_gather(stacked, "ctx", axis=0, tiled=True),
        contract_cols,
        preferred_element_type=jnp.float32,
    )
    fsdp_index = lax.axis_index("fsdp")
    features = model_width // lax.axis_size("fsdp")
    hat_mine = lax.dynamic_slice_in_dim(x_hat, fsdp_index * features, features, 1)
    gain_mine = lax.dynamic_slice_in_dim(norm_gain, fsdp_index * features, features, 0)
    d_mine = lax.psum_scatter(
        head_part.astype(jnp.bfloat16), "fsdp", scatter_dimension=1, tiled=True
    ).astype(jnp.float32)
    upstream = d_mine * gain_mine
    row_dot = lax.psum(jnp.sum(upstream * hat_mine, axis=1, keepdims=True), "fsdp")
    grad_inputs = (inv_rms * (upstream - hat_mine * row_dot / model_width)).astype(jnp.bfloat16)
    norm_row_dots = row_dot[:, 0] * float(model_width) ** (-0.5)
    gain_term = grad_scale * jnp.sum(d_mine * hat_mine, axis=0)
    weight_term = grad_scale * lax.dot_general(
        normed, d_stacked, contract_rows, preferred_element_type=jnp.float32
    )
    weight_sum, gain_sum = (
        lax.psum_scatter(
            weight_term.astype(jnp.bfloat16), "ctx", scatter_dimension=0, tiled=True
        ).astype(jnp.float32),
        lax.psum_scatter(
            gain_term.astype(jnp.bfloat16), "ctx", scatter_dimension=0, tiled=True
        ).astype(jnp.float32),
    )
    weight_sum = weight_sum.astype(jnp.bfloat16)
    q_term = grad_scale * jnp.sum(d_queries * query_normalized * query_scale, axis=(0, 1))
    k_term = grad_scale * jnp.sum(key_grads * key_normalized, axis=(0, 1))
    grad_q_gain, grad_k_gain = lax.psum((q_term, k_term), ("ctx", "fsdp"))
    return (
        grad_inputs,
        weight_sum[:, :q_cols],
        weight_sum[:, q_cols : q_cols + kv_cols],
        weight_sum[:, q_cols + kv_cols :],
        gain_sum,
        grad_q_gain,
        grad_k_gain,
        norm_row_dots,
    )


def solution(mesh):
    placed = (
        P("ctx", None),
        P("ctx", "fsdp"),
        P("ctx", "fsdp"),
        P("ctx", "fsdp"),
        P("ctx", "fsdp"),
        P(),
        P(),
        P(),
        P(),
    )
    return jax.shard_map(
        on_device,
        mesh=mesh,
        in_specs=placed,
        out_specs=(
            P("ctx", "fsdp"),
            P("ctx", "fsdp"),
            P("ctx", "fsdp"),
            P("ctx", "fsdp"),
            P(("fsdp", "ctx")),
            P(),
            P(),
            P("ctx"),
        ),
        check_vma=False,
    )
```

profile of v0, /device:TPU:0, one launch (start us, length us, event | category | flops | bytes accessed | tf_op | source)
XLA Modules:
  0.0 718.7 jit_solution(1754487045748685748)
XLA Ops:
  11.0 8.4 %copy.322 = bf16[512,5376]{0,1:T(8,128)(2,1)} copy(bf16[512,5376]{1,0:T(8,128)(2,1)} %param.21) | data formatting | bytes 11010048 | tf_op args[0]
  26.7 4.4 fusion.31
  31.7 176.1 %all-gather.2.cloned.1.call-done = bf16[5376,2048]{1,0:T(8,128)(2,1)} async-done(((bf16[672,2048]{1,0:T(8,128)(2,1)}), bf16[5376,2048]{1,0:T(8,128)(2,1)}) %all-gather.2.cloned.1.call-update) | async-done | bytes 22020112 | tf_op jit(solution)/shard_map/all_gather | solution.py:65
  207.8 17.6 %fusion.41 = f32[512,2048]{1,0:T(8,128)S(1)} fusion(bf16[5376,2048]{1,0:T(8,128)(2,1)} %all-gather.2.cloned.1.call-done, f32[5376]{0:T(1024)S(1)} %copy-done.32, f32[512]{0:T(512)S(1)} %add_rsqrt_fusion.2, bf16[512,5376]{0,1:T(8,128)(2,1)} %copy.322), kind=kOutput, calls=%fused_computation.75 | convolution fusion | flops 11285299200 | bytes 31742976 | tf_op jit(solution)/shard_map/dot_general | solution.py:63
  248.6 16.8 %conditional.6 = (f32[4,2,512]{2,1,0:T(2,128)S(1)}, f32[4,2,512,512]{2,3,1,0:T(8,128)}, f32[512,4,2,128]{0,3,2,1:T(8,128)}) conditional(s32[]{:T(128)} %convert_element_type.111, () %tuple.57, (s32[512]{0:T(512)S(1)}, s32[512,512]{0,1:T(8,128)S(1)}, s32[512]{0:T(512)S(1)}, s32[512,512]{0,1:T(8,128)S(1)}, s32[512,512]{0,1:T(8,128)S(1)}, ...), branch_computations={%region_5.6_spmd, %region_6.8_spmd} | conditional | flops 1081865216 | bytes 30958620 | solution.py:136
  249.0 5.1 fusion.51
  256.1 6.4 fusion.16
  265.4 6.2 conditional.7
  265.4 4.4 broadcast.173
  271.7 6.0 conditional.8
  271.7 4.4 broadcast.176
  277.7 4.0 multiply_reduce_fusion.2
  294.1 23.9 %conditional.9 = (f32[512,4,2,128]{3,0,2,1:T(8,128)}, f32[512,1024]{1,0:T(8,128)}) conditional(s32[]{:T(128)} %convert_element_type.111, () %tuple.56, (f32[4,2,512]{2,1,0:T(2,128)S(1)}, f32[4,2,512,512]{2,3,1,0:T(8,128)}, bf16[512,512]{1,0:T(8,128)(2,1)}, bf16[512,4,2,128]{0,3,2,1:T(8,128)(2,1)}, f32[4,2,512]{2,1,0:T(2,128)S(1)}, ...), branch_computations={%region_17.18_spmd, %region_18.19_spmd} | conditional | flops 2160590848 | bytes 70303840 | solution.py:183
  296.5 5.1 fusion.1
  303.7 4.9 fusion.2
  312.9 5.1 convolution_bitcast_fusion
  332.3 49.5 %collective-permute-done.3 = bf16[512,1024]{1,0:T(8,128)(2,1)} collective-permute-done((bf16[512,1024]{1,0:T(8,128)(2,1)}, bf16[512,1024]{1,0:T(8,128)(2,1)}, u32[]{:S(2)}, u32[]{:S(2)}) %collective-permute-start.3) | collective-permute-done | bytes 1048608 | tf_op jit(solution)/shard_map/ppermute | solution.py:17
  389.4 17.8 %convolution_convert_fusion = bf16[512,5376]{0,1:T(8,128)(2,1)} fusion(bf16[5376,2048]{1,0:T(8,128)(2,1)} %all-gather.2.cloned.1.call-done, bf16[512,512]{1,0:T(8,128)(2,1)S(1)} %copy-done.22, bf16[512,512]{1,0:T(8,128)(2,1)S(1)} %get-tuple-element.536, bf16[512,1024]{1,0:T(8,128)(2,1)S(1)} %copy-done.19), kind=kOutput, calls=%fused_computation.51 | convolution fusion | flops 11283333120 | bytes 29622272 | tf_op jit(solution)/shard_map/dot_general | solution.py:207
  408.7 19.0 %multiply_convert_fusion = bf16[5376,2048]{1,0:T(8,128)(2,1)} fusion(f32[5376]{0:T(1024)S(1)} %copy-done.33, f32[512]{0:T(512)S(1)} %copy-done.27, bf16[512,5376]{0,1:T(8,128)(2,1)} %copy.322, bf16[512,512]{1,0:T(8,128)(2,1)S(1)} %copy-done.23, bf16[512,512]{1,0:T(8,128)(2,1)S(1)} %copy-done.25, bf16[512,1024]{1,0:T(8,128)(2,1)S(1)} %copy-done.20), kind=kOutput, calls=%fused_computation.46 | convolution fusion | flops 11313610752 | bytes 29645824 | tf_op jit(solution)/shard_map/dot_general | solution.py:225
  429.6 8.2 %convert_multiply_fusion = f32[512,5376]{0,1:T(8,128)} fusion(bf16[512,5376]{0,1:T(8,128)(2,1)} %copy.322, f32[512]{0:T(512)S(1)} %copy-done.27), kind=kLoop, calls=%fused_computation.47 | loop fusion | flops 5505024 | bytes 16517120 | tf_op jit(solution)/shard_map/mul | solution.py:60
  437.9 54.0 %all-reduce.1 = (f32[128]{0:T(128)}, f32[128]{0:T(128)}) all-reduce(f32[128]{0:T(128)S(1)} %get-tuple-element.546, f32[128]{0:T(128)S(1)} %get-tuple-element.545), channel_id=1, replica_groups=mesh['ctx'=8,'fsdp'=4] {'ctx','fsdp'}, use_global_device_ids=true, to_apply=%region_32.33 | all-reduce | flops 256 | bytes 2048 | tf_op jit(solution)/shard_map/psum | solution.py:239
  495.2 10.0 %psum.21 = f32[512]{0:T(512)S(1)} all-reduce(f32[512]{0:T(512)S(1)} %get-tuple-element.512), channel_id=1, replica_groups=mesh['ctx'=8,'fsdp'=4] {'fsdp'}, use_global_device_ids=true, to_apply=%region_27.28 | all-reduce | flops 512 | bytes 4096 | tf_op jit(solution)/shard_map/psum | solution.py:221
  505.2 14.5 %all-reduce = bf16[1344]{0:T(1024)(128)(2,1)S(1)} all-reduce(bf16[1344]{0:T(1024)(128)(2,1)S(1)} %multiply_convert_fusion.7), channel_id=4, replica_groups=mesh['ctx'=8,'fsdp'=4] {'ctx'}, use_global_device_ids=true, to_apply=%region_30.31.clone | all-reduce | flops 1344 | bytes 5376
  524.4 182.6 %reduce-scatter.5.cloned.1.call-done = bf16[672,2048]{1,0:T(8,128)(2,1)} async-done(((bf16[5376,2048]{1,0:T(8,128)(2,1)}), bf16[672,2048]{1,0:T(8,128)(2,1)}) %reduce-scatter.5.cloned.1.call-update) | async-done | bytes 2752528 | tf_op jit(solution)/shard_map/reduce_scatter | solution.py:229
  (174 shorter events, 102.5 us)
Async XLA Ops:
  7.2 200.6 %all-gather.2.cloned.1.call-start = ((), (), s32[]{:S(2)}) async-start(), calls=%async_computation.2 | async-start | bytes 24772608 | tf_op jit(solution)/shard_map/all_gather | solution.py:65
  10.9 481.0 %reduce-scatter.3.cloned.1.call-start = ((), (), s32[]{:S(2)}) async-start(), calls=%async_computation.3 | async-start | bytes 6881280 | tf_op jit(solution)/shard_map/reduce_scatter | solution.py:217
  10.9 8.4 %copy-start.34 = (s32[4]{0:T(128)S(1)}, s32[4]{0:T(128)}, u32[]{:S(2)}) copy-start(s32[4]{0:T(128)} %param.29) | copy-start | bytes 52
  10.9 14.4 %copy-start.21 = (bf16[512,1024]{1,0:T(8,128)(2,1)S(1)}, bf16[512,1024]{1,0:T(8,128)(2,1)}, u32[]{:S(2)}) copy-start(bf16[512,1024]{1,0:T(8,128)(2,1)} %param.22) | copy-start | bytes 3145732
  10.9 15.7 %copy-start.35 = (f32[128]{0:T(128)S(1)}, f32[128]{0:T(128)}, u32[]{:S(2)}) copy-start(f32[128]{0:T(128)} %param.27) | copy-start | bytes 1540
  10.9 15.7 %copy-start.31 = (f32[128]{0:T(128)S(1)}, f32[128]{0:T(128)}, u32[]{:S(2)}) copy-start(f32[128]{0:T(128)} %param.28) | copy-start | bytes 1540
  19.3 188.5 %copy-start.32 = (f32[5376]{0:T(1024)S(1)}, f32[5376]{0:T(1024)}, u32[]{:S(2)}) copy-start(f32[5376]{0:T(1024)} %param.26) | copy-start | bytes 64516
  26.7 202.7 %copy-start.28 = (f32[512]{0:T(512)}, f32[512]{0:T(512)S(1)}, u32[]{:S(2)}) copy-start(f32[512]{0:T(512)S(1)} %broadcast_bitcast_fusion.1) | copy-start | bytes 6148
  31.1 194.3 %copy-start.26 = (f32[512]{0:T(512)}, f32[512]{0:T(512)S(1)}, u32[]{:S(2)}) copy-start(f32[512]{0:T(512)S(1)} %add_rsqrt_fusion.2) | copy-start | bytes 6148
  227.5 4.4 copy-start.12
  228.8 10.4 %copy-start.6 = (f32[512,2048]{1,0:T(8,128)S(1)}, f32[512,2048]{1,0:T(8,128)}, u32[]{:S(2)}) copy-start(f32[512,2048]{1,0:T(8,128)} %copy-done.5) | copy-start | bytes 12582916
  231.9 13.4 %copy-start.10 = (f32[64,4,8,128]{3,2,1,0:T(8,128)}, f32[64,4,8,128]{3,2,1,0:T(8,128)S(1)}, u32[]{:S(2)}) copy-start(f32[64,4,8,128]{3,2,1,0:T(8,128)S(1)} %get-tuple-element.537) | copy-start | bytes 3145732
  233.2 32.2 %collective-permute-start = (bf16[512,1024]{1,0:T(8,128)(2,1)}, bf16[512,1024]{1,0:T(8,128)(2,1)}, u32[]{:S(2)}, u32[]{:S(2)}) collective-permute-start(bf16[512,1024]{1,0:T(8,128)(2,1)} %pad_maximum_fusion.5), channel_id=1, source_target_pairs={{0,4},{4,8},{8,12},{12,16},{16,20},{20,24},{24,28},{1,5},{5,9},{9,... | collective-permute-start | bytes 3145736 | tf_op jit(solution)/shard_map/ppermute | solution.py:17
  236.3 35.3 %collective-permute-start.1 = (bf16[512,1024]{1,0:T(8,128)(2,1)}, bf16[512,1024]{1,0:T(8,128)(2,1)}, u32[]{:S(2)}, u32[]{:S(2)}) collective-permute-start(bf16[512,1024]{1,0:T(8,128)(2,1)} %pad_maximum_fusion.5), channel_id=1, source_target_pairs={{0,8},{4,12},{8,16},{12,20},{16,24},{20,28},{1,9},{5,13},{9,17},{1... | collective-permute-start | bytes 3145736 | tf_op jit(solution)/shard_map/ppermute | solution.py:17
  286.7 45.6 %collective-permute-start.2 = (bf16[512,1024]{1,0:T(8,128)(2,1)}, bf16[512,1024]{1,0:T(8,128)(2,1)}, u32[]{:S(2)}, u32[]{:S(2)}) collective-permute-start(bf16[512,1024]{1,0:T(8,128)(2,1)} %copy.342), channel_id=1, source_target_pairs={{4,0},{8,4},{12,8},{16,12},{20,16},{24,20},{28,24},{5,1},{9,5},{13... | collective-permute-start | bytes 3145736 | tf_op jit(solution)/shard_map/ppermute | solution.py:17
  292.8 89.0 %collective-permute-start.3 = (bf16[512,1024]{1,0:T(8,128)(2,1)}, bf16[512,1024]{1,0:T(8,128)(2,1)}, u32[]{:S(2)}, u32[]{:S(2)}) collective-permute-start(bf16[512,1024]{1,0:T(8,128)(2,1)} %copy.344), channel_id=1, source_target_pairs={{8,0},{12,4},{16,8},{20,12},{24,16},{28,20},{9,1},{13,5},{17,9},{2... | collective-permute-start | bytes 3145736 | tf_op jit(solution)/shard_map/ppermute | solution.py:17
  308.5 4.4 copy-start.15
  323.3 4.1 copy-start.30
  332.3 52.3 %copy-start.11 = (f32[64,4,8,128]{3,2,1,0:T(8,128)S(1)}, f32[64,4,8,128]{3,2,1,0:T(8,128)}, u32[]{:S(2)}) copy-start(f32[64,4,8,128]{3,2,1,0:T(8,128)} %copy-done.10) | copy-start | bytes 3145732
  381.8 5.0 copy-start.9
  381.8 5.1 copy-start.29
  386.3 3.1 copy-start.19
  407.2 299.8 %reduce-scatter.5.cloned.1.call-start = ((), (), s32[]{:S(2)}) async-start(), calls=%async_computation.4 | async-start | bytes 24772608 | tf_op jit(solution)/shard_map/reduce_scatter | solution.py:229
  491.9 29.0 %copy-start.13 = (bf16[512,1344]{0,1:T(8,128)(2,1)S(1)}, bf16[512,1344]{0,1:T(8,128)(2,1)}, u32[]{:S(2)}) copy-start(bf16[512,1344]{0,1:T(8,128)(2,1)} %reduce-scatter.3.cloned.1.call-done) | copy-start | bytes 4128772
  (18 other events, 27.2 us)
Sparse Core Ops, SparseCore 0:
  11.0 196.7 all-gather.1
  407.3 79.3 reduce-scatter.2
  489.1 217.8 reduce-scatter.4
where the time goes:
time: 727 us; the launch traced here: 719 us
  waiting for transfers between devices  408 us (56%)
  matrix products  82.5 us (11%)
  blocking collectives  78.5 us (11%)
  local copies, waits for them, and re-layouts  70.8 us (10%)
  other arithmetic  49.9 us (7%)
  between operations  19.2 us (3%)
  starting transfers between devices  8.63 us (1%)
    reduce_scatter x1, waiting for transfers between devices, on_device(): lax.psum_scatter(weight_term.astype(jnp.bfloat16), 'ctx', scatter_dimensi...  183 us
    all_gather x1, waiting for transfers between devices, on_device(): lax.all_gather(stacked, 'ctx', axis=0, tiled=True)  176 us
    psum x1, blocking collectives, on_device(): grad_q_gain, grad_k_gain = lax.psum((q_term, k_term), ('ctx', 'fsdp'))  54 us
    ppermute x4, waiting for transfers between devices, from_behind(): lax.ppermute(value, axis, [(source, source + steps) for source in range(i...  49.5 us
    unnamed x69, local copies, waits for them, and re-layouts  19.1 us
    dot_general x1, matrix products, on_device(): lax.dot_general(normed, d_stacked, contract_rows, preferred_element_type=...  19 us
    dot_general x1, matrix products, on_device(): lax.dot_general(d_stacked, lax.all_gather(stacked, 'ctx', axis=0, tiled=T...  17.8 us
    dot_general x1, matrix products, on_device(): jnp.dot(normed, lax.all_gather(stacked, 'ctx', axis=0, tiled=True), prefe...  17.6 us
  transfers between devices with their start and end apart: 7, of which 3 were waited for; matrix products, arithmetic and copies ran while one was open for 17% of the time, Pallas kernels for 0%

commit v1 on v0

v1 whole, which is shorter than its diff:
```python
import functools

import jax
import jax.numpy as jnp
from jax import lax
from jax.experimental import pallas as pl
from jax.experimental.pallas import tpu as pltpu
from jax.sharding import PartitionSpec as P

WIN = 1024
REACH = 2
BLOCKED = -1e30

epsilon = 1e-06
query_scale = 168.0 ** (-0.5)

NT = (((1,), (1,)), ((), ()))


def shift(value, axis, steps):
    count = lax.axis_size(axis)
    initial, last = (max(0, -steps), min(count, count - steps))
    return lax.ppermute(value, axis, [(s, s + steps) for s in range(initial, last)])


def swap(value, axis, flip):
    return lax.ppermute(value, axis, [(s, s ^ flip) for s in range(lax.axis_size(axis))])


def dot(a, b, dims=(((1,), (0,)), ((), ()))):
    return lax.dot_general(a, b, dims, preferred_element_type=jnp.float32)


def key_body(k_ref, v_ref, gain_ref, kv_ref):
    k = k_ref[...]
    inv = lax.rsqrt(jnp.mean(k * k, axis=1, keepdims=True) + epsilon)
    kv_ref[0] = (k * inv * gain_ref[...]).astype(jnp.bfloat16)
    kv_ref[1] = v_ref[...].astype(jnp.bfloat16)


def key_rows_of(projected, gain, kv_heads, head_dim):
    tokens = projected.shape[0]
    return pl.pallas_call(
        key_body,
        grid=(kv_heads,),
        in_specs=[
            pl.BlockSpec((tokens, head_dim), lambda g: (0, g)),
            pl.BlockSpec((tokens, head_dim), lambda g: (0, kv_heads + g)),
            pl.BlockSpec((1, head_dim), lambda g: (0, 0)),
        ],
        out_specs=pl.BlockSpec((2, tokens, head_dim), lambda g: (0, 0, g)),
        out_shape=jax.ShapeDtypeStruct((2, tokens, kv_heads * head_dim), jnp.bfloat16),
        name="key_rows",
    )(projected, projected, gain[None, :])


def key_grad_body(own_ref, near_ref, far_ref, k_ref, gain_ref, dk_ref, dv_ref, sum_ref):
    total = own_ref[...] + near_ref[...].astype(jnp.float32) + far_ref[...].astype(jnp.float32)
    k = k_ref[...]
    inv = lax.rsqrt(jnp.mean(k * k, axis=1, keepdims=True) + epsilon)
    k_hat = k * inv
    d = total[0]
    u = d * gain_ref[...]
    dk_ref[...] = (inv * (u - k_hat * jnp.mean(u * k_hat, axis=1, keepdims=True))).astype(
        jnp.bfloat16
    )
    dv_ref[...] = total[1].astype(jnp.bfloat16)

    @pl.when(pl.program_id(0) == 0)
    def _():
        sum_ref[...] = jnp.zeros_like(sum_ref)

    sum_ref[...] += jnp.sum(d * k_hat, axis=0, keepdims=True)


def key_grads_of(own, near, far, projected, gain, kv_heads, head_dim):
    tokens = projected.shape[0]
    stacked = pl.BlockSpec((2, tokens, head_dim), lambda g: (0, 0, g))
    flat = pl.BlockSpec((tokens, head_dim), lambda g: (0, g))
    row = pl.BlockSpec((1, head_dim), lambda g: (0, 0))
    half = jax.ShapeDtypeStruct((tokens, kv_heads * head_dim), jnp.bfloat16)
    return pl.pallas_call(
        key_grad_body,
        grid=(kv_heads,),
        in_specs=[stacked, stacked, stacked, flat, row],
        out_specs=(flat, flat, row),
        out_shape=(half, half, jax.ShapeDtypeStruct((1, head_dim), jnp.float32)),
        name="key_grads",
    )(own, near, far, projected, gain[None, :])


def attention_body(
    start_ref,
    ends_ref,
    q_ref,
    go_ref,
    own_ref,
    near_ref,
    far_ref,
    mult_ref,
    dq_ref,
    d_own_ref,
    d_near_ref,
    d_far_ref,
    sum_ref,
    bias_ref,
    k_ref,
    v_ref,
    kt_ref,
    vt_ref,
    dk_ref,
    dv_ref,
    *,
    rows,
    heads,
    segments,
):
    g = pl.program_id(0)
    s = pl.program_id(1)
    last = pl.num_programs(1) - 1
    tokens, head_dim = own_ref.shape[1:]
    reach = WIN
    span = reach + rows
    offset = pl.multiple_of(s * rows, rows)

    @pl.when(g == 0)
    def _():
        first = start_ref[0]
        key_pos = (first - reach + s * rows) + lax.broadcasted_iota(jnp.int32, (span, 1), 0)
        query_pos = (first + s * rows) + lax.broadcasted_iota(jnp.int32, (1, rows), 1)
        key_seg = jnp.zeros((span, 1), jnp.int32)
        query_seg = jnp.zeros((1, rows), jnp.int32)
        for i in range(segments):
            key_seg += (ends_ref[i] <= key_pos).astype(jnp.int32)
            query_seg += (ends_ref[i] <= query_pos).astype(jnp.int32)
        distance = query_pos - key_pos
        allowed = (
            (key_seg == query_seg) & (distance >= 0) & (distance < WIN) & (key_pos >= 0)
        )
        bias_ref[s] = jnp.where(allowed, 0.0, BLOCKED)

    @pl.when(s == 0)
    def _():
        for at, ref in enumerate((far_ref, near_ref, own_ref)):
            k_ref[pl.ds(at * tokens, tokens), :] = ref[0]
            v_ref[pl.ds(at * tokens, tokens), :] = ref[1]
        dk_ref[...] = jnp.zeros_like(dk_ref)
        dv_ref[...] = jnp.zeros_like(dv_ref)

    @pl.when((s == 0) & (g == 0))
    def _():
        sum_ref[...] = jnp.zeros_like(sum_ref)

    k = k_ref[pl.ds(offset, span), :]
    v = v_ref[pl.ds(offset, span), :]
    kt_ref[...] = jnp.transpose(k)
    vt_ref[...] = jnp.transpose(v)
    mult = mult_ref[...]
    bias = bias_ref[s]
    for h in range(heads):
        at = slice(h * head_dim, (h + 1) * head_dim)
        q = q_ref[:, at]
        inv = lax.rsqrt(jnp.mean(q * q, axis=1, keepdims=True) + epsilon)
        q_hat = q * inv
        q16 = (q_hat * mult).astype(jnp.bfloat16)
        go = go_ref[:, at]
        weights = jnp.exp(dot(k, q16, NT) + bias)
        over = 1.0 / jnp.sum(weights, axis=0, keepdims=True)
        out_t = dot(vt_ref[...], weights.astype(jnp.bfloat16)) * over
        delta = jnp.sum(jnp.transpose(go.astype(jnp.float32)) * out_t, axis=0, keepdims=True)
        probs = weights * over
        dv_ref[pl.ds(offset, span), :] += dot(probs.astype(jnp.bfloat16), go)
        d_scores = (probs * (dot(v, go, NT) - delta)).astype(jnp.bfloat16)
        dk_ref[pl.ds(offset, span), :] += dot(d_scores, q16)
        d_query = jnp.transpose(dot(kt_ref[...], d_scores))
        u = d_query * mult
        dq_ref[:, at] = (
            inv * (u - q_hat * jnp.mean(u * q_hat, axis=1, keepdims=True))
        ).astype(jnp.bfloat16)
        sum_ref[...] += jnp.sum(d_query * q_hat, axis=0, keepdims=True)

    @pl.when(s == last)
    def _():
        for at, ref in enumerate((d_far_ref, d_near_ref, d_own_ref)):
            ref[0] = dk_ref[pl.ds(at * tokens, tokens), :].astype(ref.dtype)
            ref[1] = dv_ref[pl.ds(at * tokens, tokens), :].astype(ref.dtype)


def attention(start, ends, q_raw, go, own, near, far, mult, kv_heads, head_dim):
    tokens, q_cols = q_raw.shape
    heads = q_cols // (kv_heads * head_dim)
    rows = min(256, tokens)
    steps = tokens // rows
    span = WIN + rows
    stacked = pl.BlockSpec((2, tokens, head_dim), lambda g, s, *_: (0, 0, g))
    by_query = pl.BlockSpec((rows, heads * head_dim), lambda g, s, *_: (s, g))
    row = pl.BlockSpec((1, head_dim), lambda g, s, *_: (0, 0))
    half = jax.ShapeDtypeStruct(own.shape, jnp.bfloat16)
    keys = WIN + tokens
    return pl.pallas_call(
        functools.partial(attention_body, rows=rows, heads=heads, segments=ends.shape[0]),
        grid_spec=pltpu.PrefetchScalarGridSpec(
            num_scalar_prefetch=2,
            grid=(kv_heads, steps),
            in_specs=[by_query, by_query, stacked, stacked, stacked, row],
            out_specs=(by_query, stacked, stacked, stacked, row),
            scratch_shapes=[
                pltpu.VMEM((steps, span, rows), jnp.float32),
                pltpu.VMEM((keys, head_dim), jnp.bfloat16),
                pltpu.VMEM((keys, head_dim), jnp.bfloat16),
                pltpu.VMEM((head_dim, span), jnp.bfloat16),
                pltpu.VMEM((head_dim, span), jnp.bfloat16),
                pltpu.VMEM((keys, head_dim), jnp.float32),
                pltpu.VMEM((keys, head_dim), jnp.float32),
            ],
        ),
        out_shape=(
            jax.ShapeDtypeStruct((tokens, q_cols), jnp.bfloat16),
            jax.ShapeDtypeStruct(own.shape, jnp.float32),
            half,
            half,
            jax.ShapeDtypeStruct((1, head_dim), jnp.float32),
        ),
        compiler_params=pltpu.CompilerParams(
            dimension_semantics=("arbitrary", "arbitrary"), vmem_limit_bytes=48 << 20
        ),
        name="attention",
    )(start, ends, q_raw, go, own, near, far, mult)


def on_device(
    inputs,
    output_cotangent,
    w_query,
    key_projection,
    value_projection,
    norm_gain,
    q_gain,
    key_norm_gain,
    half_lengths,
):
    tokens, model_width = inputs.shape
    head_dim = q_gain.shape[0]
    kv_cols = key_projection.shape[1]
    kv_heads = kv_cols // head_dim
    ctx_count = lax.axis_size("ctx")
    fsdp_count = lax.axis_size("fsdp")
    ctx_index = lax.axis_index("ctx")
    fsdp_index = lax.axis_index("fsdp")
    on_first_core = ctx_index % 2 == 0
    grad_scale = float(tokens * ctx_count) ** (-0.5)
    shard_rows = w_query.shape[0]
    features = model_width // fsdp_count

    key_value = jnp.concatenate([key_projection, value_projection], axis=1)
    wide_kv = lax.all_gather(key_value, "ctx", axis=0, tiled=True)
    wide_q = lax.all_gather(w_query, "ctx", axis=0, tiled=True)

    widened = inputs.astype(jnp.float32)
    inv_rms = lax.rsqrt(jnp.mean(widened * widened, axis=1, keepdims=True) + epsilon)
    x_hat = widened * inv_rms
    normed = (x_hat * norm_gain).astype(jnp.bfloat16)

    kv_raw = dot(normed, wide_kv)
    own = key_rows_of(kv_raw, key_norm_gain, kv_heads, head_dim)
    far = shift(own, "ctx", REACH)
    near = swap(jnp.where(on_first_core, own, far), "ctx", 1)

    q_raw = dot(normed, wide_q)
    query_multiplier = (q_gain * query_scale)[None, :]
    dq16, d_own, d_near, d_far, q_sum = attention(
        jnp.full((1,), ctx_index * tokens, jnp.int32),
        jnp.cumsum(half_lengths).astype(jnp.int32),
        q_raw,
        output_cotangent,
        own,
        near,
        far,
        query_multiplier,
        kv_heads,
        head_dim,
    )

    piece = shard_rows // fsdp_count
    blocks = jnp.transpose(normed).reshape(ctx_count, fsdp_count, piece, tokens)
    blocks = lax.dynamic_index_in_dim(blocks, fsdp_index, 1, keepdims=False)
    blocks, _ = lax.optimization_barrier((blocks, wide_q))
    blocks = lax.all_to_all(blocks, "ctx", 0, 0, tiled=True)
    blocks = jnp.transpose(blocks, (1, 0, 2)).reshape(piece, ctx_count * tokens)
    columns = lax.all_gather(blocks, "fsdp", axis=0, tiled=True)

    all_dq = lax.all_gather(dq16, "ctx", axis=0, tiled=True)

    crossed = swap(d_near, "ctx", 1)
    nothing = jnp.zeros_like(crossed)
    outgoing = d_far + jnp.where(on_first_core, nothing, crossed)
    returned = shift(outgoing, "ctx", -REACH)
    dk16, dv16, k_sum = key_grads_of(
        d_own,
        jnp.where(on_first_core, crossed, nothing),
        returned,
        kv_raw,
        key_norm_gain,
        kv_heads,
        head_dim,
    )
    dkv16 = jnp.concatenate([dk16, dv16], axis=1)
    all_dkv = lax.all_gather(dkv16, "ctx", axis=0, tiled=True)

    head_part = (dot(dq16, wide_q, NT) + dot(dkv16, wide_kv, NT)).astype(jnp.bfloat16)
    hat_gained = x_hat * norm_gain
    row_dot = lax.psum(
        jnp.sum(head_part.astype(jnp.float32) * hat_gained, axis=1, keepdims=True), "fsdp"
    )

    def part_for(index):
        return lax.dynamic_slice_in_dim(head_part, index * features, features, 1)

    d_mine = part_for(fsdp_index).astype(jnp.float32)
    for flip in range(1, fsdp_count):
        d_mine = d_mine + swap(part_for(fsdp_index ^ flip), "fsdp", flip).astype(jnp.float32)
    hat_mine = lax.dynamic_slice_in_dim(x_hat, fsdp_index * features, features, 1)
    gain_mine = lax.dynamic_slice_in_dim(norm_gain, fsdp_index * features, features, 0)
    upstream = d_mine * gain_mine
    grad_inputs = (inv_rms * (upstream - hat_mine * row_dot / model_width)).astype(jnp.bfloat16)
    norm_row_dots = row_dot[:, 0] * float(model_width) ** (-0.5)
    gain_term = grad_scale * jnp.sum(d_mine * hat_mine, axis=0)
    gain_sum = lax.psum_scatter(
        gain_term.astype(jnp.bfloat16), "ctx", scatter_dimension=0, tiled=True
    ).astype(jnp.float32)

    q_weights = (grad_scale * dot(columns, all_dq)).astype(jnp.bfloat16)
    k_weights = (grad_scale * dot(columns, all_dkv[:, :kv_cols])).astype(jnp.bfloat16)
    v_weights = (grad_scale * dot(columns, all_dkv[:, kv_cols:])).astype(jnp.bfloat16)

    grad_q_gain, grad_k_gain = lax.psum(
        (q_sum[0] * (grad_scale * query_scale), k_sum[0] * grad_scale), ("ctx", "fsdp")
    )
    return (
        grad_inputs,
        q_weights,
        k_weights,
        v_weights,
        gain_sum,
        grad_q_gain,
        grad_k_gain,
        norm_row_dots,
    )


def solution(mesh):
    placed = (
        P("ctx", None),
        P("ctx", "fsdp"),
        P("ctx", "fsdp"),
        P("ctx", "fsdp"),
        P("ctx", "fsdp"),
        P(),
        P(),
        P(),
        P(),
    )
    return jax.shard_map(
        on_device,
        mesh=mesh,
        in_specs=placed,
        out_specs=(
            P("ctx", "fsdp"),
            P("ctx", "fsdp"),
            P("ctx", "fsdp"),
            P("ctx", "fsdp"),
            P(("fsdp", "ctx")),
            P(),
            P(),
            P("ctx"),
        ),
        check_vma=False,
    )
```

time: 727 us -> 702 us (0.966)
  blocking collectives: 78.5 us -> 195 us
  waiting for transfers between devices: 408 us -> 314 us
  local copies, waits for them, and re-layouts: 70.8 us -> 34.8 us
  Pallas kernels: 0 us -> 33.9 us
  other arithmetic: 49.9 us -> 29.9 us
  matrix products: 82.5 us -> 72 us
    reduce_scatter x2 -> x0, waiting for transfers between devices: 183 us -> none  [the longest x1 183 us: on_device(): lax.psum_scatter(weight_term.astype(jnp.bfloat16), 'ctx', scatter_dimensi...]
    psum x2, blocking collectives: 64 us -> 143 us  [the longest x1 134 us: on_device(): lax.psum((q_sum[0] * (grad_scale * query_scale), k_sum[0] * grad_scale),...]
    all_gather x1 -> x5, waiting for transfers between devices: 176 us -> 236 us  [the longest x1 102 us: on_device(): wide_kv = lax.all_gather(key_value, 'ctx', axis=0, tiled=True)]
    all_to_all x0 -> x1, blocking collectives: none -> 36.4 us  [on_device(): blocks = lax.all_to_all(blocks, 'ctx', 0, 0, tiled=True)]
    pallas_call x0 -> x3, Pallas kernels: none -> 33.9 us  [the longest x1 25.4 us: attention(): pl.pallas_call(functools.partial(attention_body, rows=rows, heads=heads,...]
    ppermute x4 -> x7, waiting for transfers between devices: 49.5 us -> 76.6 us  [the longest x2 74 us: shift(): lax.ppermute(value, axis, [(s, s + steps) for s in range(initial, last)])]
    another operation x13 -> x0, local copies, waits for them, and re-layouts: 17.4 us -> none
    unnamed x69 -> x27, local copies, waits for them, and re-layouts: 19.1 us -> 5.17 us
  transfers between devices with their start and end apart: 7 -> 12, of which waited for: 3 -> 7; matrix products, arithmetic and copies ran while one was open for 17% -> 10% of each run, Pallas kernels for 0% -> 1%
where the time goes in v1:
time: 702 us; the launch traced here: 701 us
  waiting for transfers between devices  314 us (45%)
  blocking collectives  195 us (28%)
  matrix products  72 us (10%)
  local copies, waits for them, and re-layouts  34.8 us (5%)
  Pallas kernels  33.9 us (5%)
  other arithmetic  29.9 us (4%)
  between operations  14.6 us (2%)
    psum x1, blocking collectives, on_device(): lax.psum((q_sum[0] * (grad_scale * query_scale), k_sum[0] * grad_scale),...  134 us
    all_gather x1, waiting for transfers between devices, on_device(): wide_kv = lax.all_gather(key_value, 'ctx', axis=0, tiled=True)  102 us
    ppermute x2, waiting for transfers between devices, shift(): lax.ppermute(value, axis, [(s, s + steps) for s in range(initial, last)])  74 us
    dot_general x7, matrix products, dot(): return lax.dot_general(a, b, dims, preferred_element_type=jnp.float32)  72 us
    all_gather x1, waiting for transfers between devices, on_device(): all_dkv = lax.all_gather(dkv16, 'ctx', axis=0, tiled=True)  71 us
    all_gather x1, waiting for transfers between devices, on_device(): wide_q = lax.all_gather(w_query, 'ctx', axis=0, tiled=True)  55.3 us
    all_to_all x1, blocking collectives, on_device(): blocks = lax.all_to_all(blocks, 'ctx', 0, 0, tiled=True)  36.4 us
    pallas_call x1, Pallas kernels, attention(): pl.pallas_call(functools.partial(attention_body, rows=rows, heads=heads,...  25.4 us
  transfers between devices with their start and end apart: 12, of which 7 were waited for; matrix products, arithmetic and copies ran while one was open for 10% of the time, Pallas kernels for 1%

profile of v1, /device:TPU:0, one launch (start us, length us, event | category | flops | bytes accessed | tf_op | source)
XLA Modules:
  0.0 700.5 jit_solution(13463018397648926626)
XLA Ops:
  14.3 102.3 %all-gather.8.cloned.1.call-done = bf16[5376,1024]{1,0:T(8,128)(2,1)} async-done(((bf16[672,1024]{1,0:T(8,128)(2,1)}), bf16[5376,1024]{1,0:T(8,128)(2,1)}) %all-gather.8.cloned.1.call-update) | async-done | bytes 11010064 | tf_op jit(solution)/shard_map/all_gather | solution.py:256
  116.7 11.3 %fusion.18.k_ref.v_ref = f32[512,1024]{1,0:T(8,128)} fusion(bf16[5376,1024]{1,0:T(8,128)(2,1)} %all-gather.8.cloned.1.call-done, f32[5376]{0:T(1024)S(1)} %copy-done.5, f32[512]{0:T(512)S(1)} %add_rsqrt_fusion, bf16[512,5376]{1,0:T(8,128)(2,1)} %param.9), kind=kOutput, calls=%fused_computation.36 | convolution fusion | flops 5648154624 | bytes 18635776 | tf_op jit(solution)/shard_map/dot_general | solution.py:31
  128.0 3.8 key_rows.1.own_ref
  133.4 45.9 %collective-permute-done.far_ref = bf16[2,512,512]{2,1,0:T(8,128)(2,1)S(1)} collective-permute-done((bf16[2,512,512]{2,1,0:T(8,128)(2,1)}, bf16[2,512,512]{2,1,0:T(8,128)(2,1)S(1)}, u32[]{:S(2)}, u32[]{:S(2)}) %collective-permute-start) | collective-permute-done | bytes 1048608 | tf_op jit(solution)/shard_map/ppermute | solution.py:23
  182.0 55.3 %all-gather.6.cloned.1.call-done = bf16[5376,1024]{1,0:T(8,128)(2,1)} async-done(((bf16[672,1024]{1,0:T(8,128)(2,1)}), bf16[5376,1024]{1,0:T(8,128)(2,1)}) %all-gather.6.cloned.1.call-update) | async-done | bytes 11010064 | tf_op jit(solution)/shard_map/all_gather | solution.py:257
  237.2 11.3 %fusion.19.q_ref = f32[512,1024]{1,0:T(8,128)} fusion(bf16[5376,1024]{1,0:T(8,128)(2,1)} %all-gather.6.cloned.1.call-done, f32[5376]{0:T(1024)S(1)} %copy-done.5, f32[512]{0:T(512)S(1)} %add_rsqrt_fusion, bf16[512,5376]{1,0:T(8,128)(2,1)} %param.9), kind=kOutput, calls=%fused_computation.37 | convolution fusion | flops 5648154624 | bytes 18635776 | tf_op jit(solution)/shard_map/dot_general | solution.py:31
  248.6 25.4 %attention.1 = (bf16[512,1024]{1,0:T(8,128)(2,1)}, f32[2,512,512]{2,1,0:T(8,128)}, bf16[2,512,512]{2,1,0:T(8,128)(2,1)S(1)}, bf16[2,512,512]{2,1,0:T(8,128)(2,1)S(1)}, f32[1,128]{1,0:T(1,128)S(1)}) custom-call(s32[1]{0:T(128)} %bitcast.start_ref, s32[4]{0:T(128)S(1)} %bitcast.29, f32[512,1024]{1,0:T(8,128)} %fusion.19.q_ref, ...), custom_call_target="tpu_custom_call" | custom-call | tf_op jit(solution)/shard_map/attention/pallas_call | solution.py:200
  279.2 28.0 %collective-permute-done.3.far_ref = bf16[2,512,512]{2,1,0:T(8,128)(2,1)S(1)} collective-permute-done((bf16[2,512,512]{2,1,0:T(8,128)(2,1)S(1)}, bf16[2,512,512]{2,1,0:T(8,128)(2,1)S(1)}, u32[]{:S(2)}, u32[]{:S(2)}) %collective-permute-start.3) | collective-permute-done | bytes 1048608 | tf_op jit(solution)/shard_map/ppermute | solution.py:23
  308.2 4.7 key_grads.1
  315.1 13.0 %fusion.20 = f32[512,5376]{1,0:T(8,128)} fusion(bf16[512,1024]{1,0:T(8,128)(2,1)S(1)} %constant_dynamic-update-slice_fusion, bf16[5376,1024]{1,0:T(8,128)(2,1)} %all-gather.8.cloned.1.call-done), kind=kOutput, calls=%fused_computation.38 | convolution fusion | flops 5637144576 | bytes 23068672 | tf_op jit(solution)/shard_map/dot_general | solution.py:31
  328.1 13.6 %add_convert_fusion = bf16[512,5376]{1,0:T(8,128)(2,1)} fusion(f32[512,5376]{1,0:T(8,128)} %fusion.20, bf16[512,1024]{1,0:T(8,128)(2,1)} %get-tuple-element.17, bf16[5376,1024]{1,0:T(8,128)(2,1)} %all-gather.6.cloned.1.call-done), kind=kOutput, calls=%fused_computation.4 | convolution fusion | flops 5642649600 | bytes 28573696 | tf_op jit(solution)/shard_map/dot_general | solution.py:31
  341.7 12.3 %fusion.17 = (bf16[5376,512]{0,1:T(8,128)(2,1)}, f32[512]{0:T(512)S(1)}, f32[512,5376]{1,0:T(8,128)}) fusion(f32[5376]{0:T(1024)S(1)} %copy-done.5, f32[512]{0:T(512)S(1)} %add_rsqrt_fusion, bf16[512,5376]{1,0:T(8,128)(2,1)} %param.9, bf16[512,5376]{1,0:T(8,128)(2,1)} %add_convert_fusion), kind=kLoop, calls=%fused_computation.35 | loop fusion | flops 19267072 | bytes 27550720 | tf_op jit(solution)/shard_map/transpose | solution.py:285
  354.0 8.3 %copy.27 = bf16[5376,512]{1,0:T(8,128)(2,1)} copy(bf16[5376,512]{0,1:T(8,128)(2,1)} %get-tuple-element.54) | data formatting | bytes 11010048 | tf_op jit(solution)/shard_map/transpose | solution.py:285
  363.8 36.4 %all_to_all.5 = bf16[8,168,512]{2,1,0:T(8,128)(2,1)S(1)} all-to-all(bf16[8,168,512]{2,1,0:T(8,128)(2,1)S(1)} %dynamic-slice_bitcast_fusion), channel_id=1, replica_groups=mesh['ctx'=8,'fsdp'=4] {'ctx'}, dimensions={0} | all-to-all | bytes 2752512 | tf_op jit(solution)/shard_map/all_to_all | solution.py:288
  402.7 5.6 constant_dynamic-slice_fusion.2
  418.7 133.8 %all-reduce.1 = (f32[128]{0:T(128)}, f32[128]{0:T(128)}) all-reduce(f32[128]{0:T(128)S(1)} %multiply_bitcast_fusion.1, f32[128]{0:T(128)S(1)} %multiply_bitcast_fusion), channel_id=1, replica_groups=mesh['ctx'=8,'fsdp'=4] {'ctx','fsdp'}, use_global_device_ids=true, to_apply=%region_6.7 | all-reduce | flops 256 | bytes 2048 | tf_op jit(solution)/shard_map/psum | solution.py:336
  552.5 9.7 %psum.21 = f32[512]{0:T(512)S(1)} all-reduce(f32[512]{0:T(512)S(1)} %get-tuple-element.55), channel_id=1, replica_groups=mesh['ctx'=8,'fsdp'=4] {'fsdp'}, use_global_device_ids=true, to_apply=%region_3.4 | all-reduce | flops 512 | bytes 4096 | tf_op jit(solution)/shard_map/psum | solution.py:312
  569.0 6.2 multiply_reduce_fusion.1
  577.7 14.9 %all-reduce = bf16[1344]{0:T(1024)(128)(2,1)S(1)} all-reduce(bf16[1344]{0:T(1024)(128)(2,1)S(1)} %multiply_convert_fusion.3), channel_id=2, replica_groups=mesh['ctx'=8,'fsdp'=4] {'ctx'}, use_global_device_ids=true, to_apply=%region_5.6.clone | all-reduce | flops 1344 | bytes 5376
  593.2 7.0 %all-gather.12.cloned.1.call-done = bf16[4096,1024]{1,0:T(8,128)(2,1)} async-done(((bf16[512,1024]{1,0:T(8,128)(2,1)}), bf16[4096,1024]{1,0:T(8,128)(2,1)}) %all-gather.12.cloned.1.call-update) | async-done | bytes 8388624 | tf_op jit(solution)/shard_map/all_gather | solution.py:292
  600.3 11.1 %multiply_convert_fusion.2 = bf16[672,1024]{1,0:T(8,128)(2,1)} fusion(bf16[672,4096]{1,0:T(8,128)(2,1)} %all-gather.10.cloned.1.call-done, bf16[4096,1024]{1,0:T(8,128)(2,1)} %all-gather.12.cloned.1.call-done), kind=kOutput, calls=%fused_computation.13 | convolution fusion | flops 5638520832 | bytes 15269888 | tf_op jit(solution)/shard_map/dot_general | solution.py:31
  611.4 71.0 %all-gather.14.cloned.1.call-done = bf16[4096,1024]{1,0:T(8,128)(2,1)} async-done(((bf16[512,1024]{1,0:T(8,128)(2,1)}), bf16[4096,1024]{1,0:T(8,128)(2,1)}) %all-gather.14.cloned.1.call-update) | async-done | bytes 8388624 | tf_op jit(solution)/shard_map/all_gather | solution.py:308
  682.3 7.8 %fusion.11 = bf16[672,512]{1,0:T(8,128)(2,1)} fusion(bf16[672,4096]{1,0:T(8,128)(2,1)} %all-gather.10.cloned.1.call-done, bf16[4096,1024]{1,0:T(8,128)(2,1)} %all-gather.14.cloned.1.call-done), kind=kOutput, calls=%fused_computation.18 | convolution fusion | flops 2819260416 | bytes 10387456 | tf_op jit(solution)/shard_map/dot_general | solution.py:31
  690.1 3.9 fusion.14
  (72 shorter events, 43.4 us)
Async XLA Ops:
  7.2 109.5 %copy-start.5 = (f32[5376]{0:T(1024)S(1)}, f32[5376]{0:T(1024)}, u32[]{:S(2)}) copy-start(f32[5376]{0:T(1024)} %param.14) | copy-start | bytes 64516
  7.2 109.5 %all-gather.8.cloned.1.call-start = ((), (), s32[]{:S(2)}) async-start(), calls=%async_computation.2 | async-start | bytes 12386304 | tf_op jit(solution)/shard_map/all_gather | solution.py:256
  9.8 227.4 %all-gather.6.cloned.1.call-start = ((), (), s32[]{:S(2)}) async-start(), calls=%async_computation.1 | async-start | bytes 12386304 | tf_op jit(solution)/shard_map/all_gather | solution.py:257
  10.5 582.7 %all-gather.10.cloned.1.call-start = ((), (), s32[]{:S(2)}) async-start(), calls=%async_computation.3 | async-start | bytes 6881280 | tf_op jit(solution)/shard_map/all_gather | solution.py:290
  14.3 118.8 %copy-start.8 = (s32[4]{0:T(128)S(1)}, s32[4]{0:T(128)}, u32[]{:S(2)}) copy-start(s32[4]{0:T(128)} %param.17) | copy-start | bytes 52
  14.3 119.0 %copy-start.9 = (f32[128]{0:T(128)S(1)}, f32[128]{0:T(128)}, u32[]{:S(2)}) copy-start(f32[128]{0:T(128)} %param.15) | copy-start | bytes 1540
  131.8 47.5 %collective-permute-start = (bf16[2,512,512]{2,1,0:T(8,128)(2,1)}, bf16[2,512,512]{2,1,0:T(8,128)(2,1)S(1)}, u32[]{:S(2)}, u32[]{:S(2)}) collective-permute-start(bf16[2,512,512]{2,1,0:T(8,128)(2,1)} %key_rows.1.own_ref), channel_id=1, source_target_pairs={{0,8},{4,12},{8,16},{12,20},{16,24},{20,28},{1,9},{5,13},{9,17},{1... | collective-permute-start | bytes 3145736 | tf_op jit(solution)/shard_map/ppermute | solution.py:23
  179.3 69.3 %copy-start.2 = (bf16[2,512,512]{2,1,0:T(8,128)(2,1)}, bf16[2,512,512]{2,1,0:T(8,128)(2,1)S(1)}, u32[]{:S(2)}) copy-start(bf16[2,512,512]{2,1,0:T(8,128)(2,1)S(1)} %collective-permute-done.far_ref) | copy-start | bytes 3145732
  182.0 66.6 %copy-start = (bf16[2,512,512]{2,1,0:T(8,128)(2,1)S(1)}, bf16[2,512,512]{2,1,0:T(8,128)(2,1)}, u32[]{:S(2)}) copy-start(bf16[2,512,512]{2,1,0:T(8,128)(2,1)} %key_rows.1.own_ref) | copy-start | bytes 3145732
  182.0 66.6 %copy-start.1 = (bf16[512,1024]{1,0:T(8,128)(2,1)S(1)}, bf16[512,1024]{1,0:T(8,128)(2,1)}, u32[]{:S(2)}) copy-start(bf16[512,1024]{1,0:T(8,128)(2,1)} %go_ref.1) | copy-start | bytes 3145732
  182.0 66.6 %collective-permute-start.1 = (bf16[2,512,512]{2,1,0:T(8,128)(2,1)}, bf16[2,512,512]{2,1,0:T(8,128)(2,1)}, u32[]{:S(2)}, u32[]{:S(2)}) collective-permute-start(bf16[2,512,512]{2,1,0:T(8,128)(2,1)} %broadcast_select_fusion.1), channel_id=1, source_target_pairs={{0,4},{4,0},{8,12},{12,8},{16,20},{20,16},{24,28},{28,24},{1,5},{5... | collective-permute-start | bytes 3145736 | tf_op jit(solution)/shard_map/ppermute | solution.py:27
  274.0 2.7 collective-permute-start.2
  277.7 29.5 %collective-permute-start.3 = (bf16[2,512,512]{2,1,0:T(8,128)(2,1)S(1)}, bf16[2,512,512]{2,1,0:T(8,128)(2,1)S(1)}, u32[]{:S(2)}, u32[]{:S(2)}) collective-permute-start(bf16[2,512,512]{2,1,0:T(8,128)(2,1)S(1)} %get-tuple-element.60), channel_id=1, source_target_pairs={{8,0},{12,4},{16,8},{20,12},{24,16},{28,20},{9,1},{13,5},{17,9},{2... | collective-permute-start | bytes 3145736 | tf_op jit(solution)/shard_map/ppermute | solution.py:23
  307.2 1.0 copy-start.4
  315.1 13.0 %copy-start.3 = (bf16[512,1024]{1,0:T(8,128)(2,1)}, bf16[512,1024]{1,0:T(8,128)(2,1)S(1)}, u32[]{:S(2)}) copy-start(bf16[512,1024]{1,0:T(8,128)(2,1)S(1)} %constant_dynamic-update-slice_fusion) | copy-start | bytes 3145732
  401.5 198.8 %all-gather.12.cloned.1.call-start = ((), (), s32[]{:S(2)}) async-start(), calls=%async_computation.4 | async-start | bytes 9437184 | tf_op jit(solution)/shard_map/all_gather | solution.py:292
  402.1 280.3 %all-gather.14.cloned.1.call-start = ((), (), s32[]{:S(2)}) async-start(), calls=%async_computation.5 | async-start | bytes 9437184 | tf_op jit(solution)/shard_map/all_gather | solution.py:308
  408.2 9.2 %copy-start.11 = (u32[32]{0:T(128)S(1)}, u32[32]{0:T(128)}, u32[]{:S(2)}) copy-start(u32[32]{0:T(128)} %constant.64) | copy-start | bytes 388
  408.2 10.5 %copy-start.10 = (f32[1,128]{1,0:T(1,128)S(1)}, f32[1,128]{1,0:T(1,128)}, u32[]{:S(2)}) copy-start(f32[1,128]{1,0:T(1,128)} %get-tuple-element.25) | copy-start | bytes 1540
  410.9 151.9 %collective-permute-start.4 = (bf16[512,1344]{0,1:T(8,128)(2,1)}, bf16[512,1344]{0,1:T(8,128)(2,1)}, u32[]{:S(2)}, u32[]{:S(2)}) collective-permute-start(bf16[512,1344]{0,1:T(8,128)(2,1)} %copy.21), channel_id=1, source_target_pairs={{0,1},{1,0},{2,3},{3,2},{4,5},{5,4},{6,7},{7,6},{8,9},{9,8},{10,11... | collective-permute-start | bytes 4128776 | tf_op jit(solution)/shard_map/ppermute | solution.py:27
  414.1 150.5 %collective-permute-start.5 = (bf16[512,1344]{0,1:T(8,128)(2,1)}, bf16[512,1344]{0,1:T(8,128)(2,1)}, u32[]{:S(2)}, u32[]{:S(2)}) collective-permute-start(bf16[512,1344]{0,1:T(8,128)(2,1)} %copy.23), channel_id=1, source_target_pairs={{0,2},{1,3},{2,0},{3,1},{4,6},{5,7},{6,4},{7,5},{8,10},{9,11},{10,... | collective-permute-start | bytes 4128776 | tf_op jit(solution)/shard_map/ppermute | solution.py:27
  417.1 149.3 %collective-permute-start.6 = (bf16[512,1344]{0,1:T(8,128)(2,1)}, bf16[512,1344]{0,1:T(8,128)(2,1)}, u32[]{:S(2)}, u32[]{:S(2)}) collective-permute-start(bf16[512,1344]{0,1:T(8,128)(2,1)} %copy.25), channel_id=1, source_target_pairs={{0,3},{1,2},{2,1},{3,0},{4,7},{5,6},{6,5},{7,4},{8,11},{9,10},{10,... | collective-permute-start | bytes 4128776 | tf_op jit(solution)/shard_map/ppermute | solution.py:27
  682.3 7.8 %copy-start.6 = (bf16[4096,1024]{1,0:T(8,128)(2,1)S(1)}, bf16[4096,1024]{1,0:T(8,128)(2,1)}, u32[]{:S(2)}) copy-start(bf16[4096,1024]{1,0:T(8,128)(2,1)} %all-gather.14.cloned.1.call-done) | copy-start | bytes 25165828
  682.3 7.8 %copy-start.7 = (bf16[672,4096]{1,0:T(8,128)(2,1)S(1)}, bf16[672,4096]{1,0:T(8,128)(2,1)}, u32[]{:S(2)}) copy-start(bf16[672,4096]{1,0:T(8,128)(2,1)} %all-gather.10.cloned.1.call-done) | copy-start | bytes 16515076
Sparse Core Ops, SparseCore 0:
  10.2 106.4 all-gather.7
  118.3 118.8 all-gather.5
  401.6 106.8 all-gather.9
  510.0 90.2 all-gather.11
  601.7 80.5 all-gather.13
